TPU v7x, 32 devices: a whole 2x2x4 slice. The times are simulated.
32 devices in a mesh: frame: 8 (over z, core), tok: 4 (over y, x).
Axes of the slice: x: 2, y: 2, z: 4, core: 2. Of those that a mesh axis runs over, the one named last changes fastest.
Arguments:
- stream: bfloat16 [8, 1024, 1152], P('frame', 'tok'), may hold values from -20 to 20
- queries: bfloat16 [8, 1024, 1152], P('frame', 'tok'), may hold values from -200 to 200
- key_vectors: bfloat16 [8, 1024, 1152], P('frame', 'tok'), may hold values from -6 to 6
- value_vectors: bfloat16 [8, 1024, 1152], P('frame', 'tok'), may hold values from -6 to 6
- modulation: float32 [8, 4, 1152], P('frame'), may hold values from -4 to 4
- output_weight: bfloat16 [1152, 1152], replicated, may hold values from -0.1875 to 0.1875
- output_bias: float32 [1152], replicated, may hold values from -3 to 3
- router_weight: bfloat16 [1152, 8], replicated, may hold values from -0.1875 to 0.1875
- expand_weight: bfloat16 [8, 1152, 4608], P('frame', None, 'tok'), may hold values from -0.1875 to 0.1875
- expand_bias: float32 [8, 4608], P('frame', 'tok'), may hold values from -3 to 3
- reduce_weight: bfloat16 [8, 4608, 1152], P('frame', 'tok'), may hold values from -0.09375 to 0.09375
- reduce_bias: float32 [8, 1152], P('frame'), may hold values from -3 to 3
- counts: int32 [8, 8], P(None, 'frame'), may hold values from 1 to 96, 256 in all within a row
- picked_rows: int32 [8, 8, 96], P(None, 'frame'), may hold values from 0 to 1023, as said below
Outputs:
- layer_out: bfloat16 [8, 1024, 1152], P('frame', 'tok')
Inputs may be any that keep to these rules, and one draw needn't show every extreme that they name: counts[e, g] slots of block (e, g) are used; the counts of one expert sum to 256. The entries of one block picked_rows[e, g, :] are distinct positions among the 1024 tokens of frame g; slots at or beyond counts[e, g] are unused.
All inputs are finite; a program needn't handle non-finite values.
Results may differ from a plain program's by a relative error of at most 0.0055.
Values may be sent and summed in bfloat16 or wider, within the bound.
A program may use at most 64 MiB of HBM per device.

v0:
```python
import math
import jax
import jax.numpy as jnp
from jax import lax
from jax.sharding import PartitionSpec as P

H = 16
HD = 72


def layer_norm(values):
    mean_val = jnp.mean(values, axis=-1, keepdims=True)
    centred = values - mean_val
    variance = jnp.mean(centred * centred, axis=-1, keepdims=True)
    return centred * lax.rsqrt(variance + 1e-06)


def head_attention(operands):
    head_queries, head_keys, head_values = operands
    length = head_queries.shape[1]
    block_rows = min(512, length)
    score_scale = 1.0 / math.sqrt(HD)

    def one_block(first_row):
        query_block = lax.dynamic_slice_in_dim(head_queries, first_row, block_rows, 1)
        scores = (
            lax.dot_general(
                query_block, head_keys, (((0,), (0,)), ((), ())), preferred_element_type=jnp.float32
            )
            * score_scale
        )
        scores = scores - jnp.max(scores, axis=1, keepdims=True)
        exponent = jnp.exp(scores)
        weights = (exponent / jnp.sum(exponent, axis=1, keepdims=True)).astype(jnp.bfloat16)
        return lax.dot_general(
            head_values, weights, (((1,), (1,)), ((), ())), preferred_element_type=jnp.float32
        ).astype(jnp.bfloat16)

    starts = jnp.arange(length // block_rows, dtype=jnp.int32) * block_rows
    blocks = lax.map(one_block, starts)
    return blocks.transpose(1, 0, 2).reshape(head_queries.shape[0], length)


def attend_items(pieces):
    outputs = lax.map(head_attention, (pieces[0][0], pieces[1][0], pieces[2][0]))
    return outputs[None]


def per_device(
    stream,
    queries,
    key_vectors,
    value_vectors,
    modulation,
    output_weight,
    output_bias,
    router_weight,
    expand_weight,
    expand_bias,
    reduce_weight,
    reduce_bias,
    counts,
    picked_rows,
):
    tok_groups = lax.axis_size("tok")
    tok_local = stream.shape[1]
    model_width = stream.shape[2]
    heads_local = H // tok_groups

    def to_heads(tensor):
        return tensor[0].reshape(tok_local, tok_groups, heads_local, HD).transpose(1, 2, 3, 0)

    attended = attend_items(
        (
            lax.all_to_all(to_heads(queries), "tok", split_axis=0, concat_axis=3, tiled=True),
            lax.all_to_all(to_heads(key_vectors), "tok", split_axis=0, concat_axis=3, tiled=True),
            lax.all_to_all(to_heads(value_vectors), "tok", split_axis=0, concat_axis=3, tiled=True),
        )
    )
    returned = lax.all_to_all(attended, "tok", split_axis=3, concat_axis=0, tiled=True)
    attended_rows = returned.transpose(3, 0, 1, 2).reshape(tok_local, model_width)
    projected = (
        jnp.dot(attended_rows, output_weight, preferred_element_type=jnp.float32) + output_bias
    )
    shares = modulation[0]
    residual = (stream[0].astype(jnp.float32) + shares[0] * projected).astype(jnp.bfloat16)
    normed = (layer_norm(residual.astype(jnp.float32)) * (1.0 + shares[2]) + shares[1]).astype(
        jnp.bfloat16
    )
    gate_values = jax.nn.sigmoid(jnp.dot(normed, router_weight, preferred_element_type=jnp.float32))
    slot_count = picked_rows.shape[2]
    local_pos = picked_rows[:, 0, :] - lax.axis_index("tok") * tok_local
    in_use = jnp.arange(slot_count, dtype=jnp.int32)[None, :] < counts
    on_shard = in_use & (local_pos >= 0) & (local_pos < tok_local)
    safe_pos = jnp.clip(local_pos, 0, tok_local - 1)
    chosen = jnp.take(normed, safe_pos, axis=0)
    chosen = jnp.where(on_shard[:, :, None], chosen, jnp.zeros_like(chosen))
    moved = lax.all_to_all(chosen, "frame", split_axis=0, concat_axis=1, tiled=True)
    expert_rows = lax.psum(moved.astype(jnp.float32).astype(jnp.bfloat16), "tok")
    hidden = jax.nn.gelu(
        jnp.einsum("erd,edf->erf", expert_rows, expand_weight, preferred_element_type=jnp.float32)
        + expand_bias[:, None, :],
        approximate=True,
    ).astype(jnp.bfloat16)
    partial_out = jnp.einsum(
        "erf,efd->erd", hidden, reduce_weight, preferred_element_type=jnp.float32
    )
    column_count = model_width // tok_groups
    summed = lax.psum_scatter(
        partial_out.astype(jnp.bfloat16), "tok", scatter_dimension=2, tiled=True
    ).astype(jnp.float32)
    bias_part = lax.dynamic_slice_in_dim(
        reduce_bias, lax.axis_index("tok") * column_count, column_count, 1
    )
    expert_out = (summed + bias_part[:, None, :]).astype(jnp.bfloat16)
    returned_cols = lax.all_to_all(expert_out, "frame", split_axis=1, concat_axis=0, tiled=True)
    returned_rows = lax.all_gather(returned_cols, "tok", axis=2, tiled=True)
    mix_weight = jnp.take_along_axis(gate_values.T, safe_pos, axis=1)
    mix_weight = jnp.where(on_shard, mix_weight, jnp.zeros_like(mix_weight)).astype(jnp.bfloat16)
    targets = jnp.arange(tok_local, dtype=jnp.int32)
    matches = (safe_pos.reshape(-1)[None, :] == targets[:, None]) & on_shard.reshape(-1)[None, :]
    scatter_table = jnp.where(matches, mix_weight.reshape(-1)[None, :], jnp.zeros((), jnp.bfloat16))
    expert_mix = jnp.dot(
        scatter_table, returned_rows.reshape(-1, model_width), preferred_element_type=jnp.float32
    )
    layer_out = (residual.astype(jnp.float32) + shares[3] * expert_mix).astype(jnp.bfloat16)
    return layer_out[None]


def solution(mesh):
    return jax.shard_map(
        per_device,
        mesh=mesh,
        in_specs=(
            P("frame", "tok", None),
            P("frame", "tok", None),
            P("frame", "tok", None),
            P("frame", "tok", None),
            P("frame", None, None),
            P(),
            P(),
            P(),
            P("frame", None, "tok"),
            P("frame", "tok"),
            P("frame", "tok", None),
            P("frame", None),
            P(None, "frame"),
            P(None, "frame", None),
        ),
        out_specs=P("frame", "tok", None),
        check_vma=False,
    )
```

profile of v0, /device:TPU:0, one launch (start us, length us, event | category | flops | bytes accessed | tf_op | source)
XLA Modules:
  0.0 382.8 jit_solution(11425842389973880382)
XLA Ops:
  8.8 5.2 %all-to-all-start = ((bf16[4,4,72,256]{3,2,1,0:T(8,128)(2,1)}), bf16[4,4,72,256]{3,2,1,0:T(8,128)(2,1)S(1)}, u32[]{:S(2)}, u32[]{:S(2)}) async-start(bf16[4,4,72,256]{3,2,1,0:T(8,128)(2,1)} %bitcast.128), calls=%async_computation | async-start | bytes 1179648 | tf_op jit(solution)/shard_map/all_to_all | solution.py:75
  16.1 6.6 %all-to-all-done = bf16[4,4,72,256]{3,2,1,0:T(8,128)(2,1)S(1)} async-done(((bf16[4,4,72,256]{3,2,1,0:T(8,128)(2,1)}), bf16[4,4,72,256]{3,2,1,0:T(8,128)(2,1)S(1)}, u32[]{:S(2)}, u32[]{:S(2)}) %all-to-all-start) | async-done | bytes 589856 | tf_op jit(solution)/shard_map/all_to_all | solution.py:75
  22.7 4.3 %all-to-all-start.1 = ((bf16[4,4,72,256]{3,2,1,0:T(8,128)(2,1)}), bf16[4,4,72,256]{3,2,1,0:T(8,128)(2,1)}, u32[]{:S(2)}, u32[]{:S(2)}) async-start(bf16[4,4,72,256]{3,2,1,0:T(8,128)(2,1)} %bitcast.127), calls=%async_computation.1 | async-start | bytes 1179648 | tf_op jit(solution)/shard_map/all_to_all | solution.py:76
  29.2 5.9 %all-to-all-done.1 = bf16[4,4,72,256]{3,2,1,0:T(8,128)(2,1)} async-done(((bf16[4,4,72,256]{3,2,1,0:T(8,128)(2,1)}), bf16[4,4,72,256]{3,2,1,0:T(8,128)(2,1)}, u32[]{:S(2)}, u32[]{:S(2)}) %all-to-all-start.1) | async-done | bytes 589856 | tf_op jit(solution)/shard_map/all_to_all | solution.py:76
  35.1 4.2 %all-to-all-start.2 = ((bf16[4,4,72,256]{3,2,1,0:T(8,128)(2,1)}), bf16[4,4,72,256]{3,2,1,0:T(8,128)(2,1)}, u32[]{:S(2)}, u32[]{:S(2)}) async-start(bf16[4,4,72,256]{3,2,1,0:T(8,128)(2,1)} %bitcast.126), calls=%async_computation.2 | async-start | bytes 1179648 | tf_op jit(solution)/shard_map/all_to_all | solution.py:77
  40.8 2.4 squeeze.27
  49.6 45.9 %while.21 = (s32[]{:T(128)}, bf16[4,72,1024]{2,1,0:T(8,128)(2,1)}, bf16[4,72,1024]{2,1,0:T(8,128)(2,1)}, bf16[4,72,1024]{2,1,0:T(8,128)(2,1)}, bf16[4,72,1024]{2...) while((s32[]{:T(128)}, bf16[4,72,1024]{2,1,0:T(8,128)(2,1)}, ...), condition=%wide.region_5.6_spmd, body=%wide.region_0.5_spmd.sunk | while | flops 155749376 | bytes 8513900 | solution.py:45
  51.6 8.6 %while.22 = (s32[]{:T(128)}, bf16[2,72,512]{2,1,0:T(8,128)(2,1)S(1)}, s32[2]{0:T(128)S(1)}, bf16[72,1024]{1,0:T(8,128)(2,1)S(1)}, bf16[72,1024]{1,0:T(8,128)(2,1...) while((s32[]{:T(128)}, bf16[2,72,512]{2,1,0:T(8,128)(2,1)S(1)}, ...), condition=%wide.region_4.4_spmd, body=%wide.region_1.3_spmd.sunk | while | flops 155749376 | bytes 6744219 | solution.py:40
  63.1 8.6 %while.22 = (s32[]{:T(128)}, bf16[2,72,512]{2,1,0:T(8,128)(2,1)S(1)}, s32[2]{0:T(128)S(1)}, bf16[72,1024]{1,0:T(8,128)(2,1)S(1)}, bf16[72,1024]{1,0:T(8,128)(2,1...) while((s32[]{:T(128)}, bf16[2,72,512]{2,1,0:T(8,128)(2,1)S(1)}, ...), condition=%wide.region_4.4_spmd, body=%wide.region_1.3_spmd.sunk | while | flops 155749376 | bytes 6744219 | solution.py:40
  74.6 8.6 %while.22 = (s32[]{:T(128)}, bf16[2,72,512]{2,1,0:T(8,128)(2,1)S(1)}, s32[2]{0:T(128)S(1)}, bf16[72,1024]{1,0:T(8,128)(2,1)S(1)}, bf16[72,1024]{1,0:T(8,128)(2,1...) while((s32[]{:T(128)}, bf16[2,72,512]{2,1,0:T(8,128)(2,1)S(1)}, ...), condition=%wide.region_4.4_spmd, body=%wide.region_1.3_spmd.sunk | while | flops 155749376 | bytes 6744219 | solution.py:40
  86.0 8.6 %while.22 = (s32[]{:T(128)}, bf16[2,72,512]{2,1,0:T(8,128)(2,1)S(1)}, s32[2]{0:T(128)S(1)}, bf16[72,1024]{1,0:T(8,128)(2,1)S(1)}, bf16[72,1024]{1,0:T(8,128)(2,1...) while((s32[]{:T(128)}, bf16[2,72,512]{2,1,0:T(8,128)(2,1)S(1)}, ...), condition=%wide.region_4.4_spmd, body=%wide.region_1.3_spmd.sunk | while | flops 155749376 | bytes 6744219 | solution.py:40
  97.9 4.4 %all-to-all-start.3 = ((bf16[1,4,72,1024]{2,1,0,3:T(4,128)(2,1)}), bf16[1,4,72,1024]{2,1,0,3:T(4,128)(2,1)}, u32[]{:S(2)}, u32[]{:S(2)}) async-start(bf16[1,4,72,1024]{2,1,0,3:T(4,128)(2,1)} %bitcast.123), calls=%async_computation.3 | async-start | bytes 2097152 | tf_op jit(solution)/shard_map/all_to_all | solution.py:80
  102.5 11.4 %all-to-all-done.3 = bf16[1,4,72,1024]{2,1,0,3:T(4,128)(2,1)} async-done(((bf16[1,4,72,1024]{2,1,0,3:T(4,128)(2,1)}), bf16[1,4,72,1024]{2,1,0,3:T(4,128)(2,1)}, u32[]{:S(2)}, u32[]{:S(2)}) %all-to-all-start.3) | async-done | bytes 589856 | tf_op jit(solution)/shard_map/all_to_all | solution.py:80
  115.4 3.0 fusion.44
  119.7 3.7 gather_fusion
  125.3 46.8 %all_to_all.87 = bf16[8,96,1152]{2,1,0:T(8,128)(2,1)} all-to-all(bf16[8,96,1152]{2,1,0:T(8,128)(2,1)S(1)} %select_select_fusion), channel_id=1, replica_groups=mesh['frame'=8,'tok'=4] {'frame'}, dimensions={0} | all-to-all | bytes 3538944 | tf_op jit(solution)/shard_map/all_to_all | solution.py:98
  172.8 61.5 %all-reduce.2.cloned.1.call-done = bf16[768,1152]{1,0:T(8,128)(2,1)} async-done(((bf16[768,1152]{1,0:T(8,128)(2,1)}), bf16[768,1152]{1,0:T(8,128)(2,1)}) %all-reduce.2.cloned.1.call-update) | async-done | bytes 1769488 | tf_op jit(solution)/shard_map/psum | solution.py:99
  234.2 8.8 %fusion.15 = bf16[1,768,1152]{2,1,0:T(8,128)(2,1)} fusion(bf16[1,1152,1152]{2,1,0:T(8,128)(2,1)S(1)} %copy-done, bf16[768,1152]{1,0:T(8,128)(2,1)} %all-reduce.2.cloned.1.call-done, bf16[1,1152,1152]{2,1,0:T(8,128)(2,1)} %param.26, f32[1152]{0:T(1024)S(1)} %reduce.5), kind=kOutput, calls=%fused_computation.29 | convolution fusion | flops 4086595584 | bytes 8851968 | tf_op jit(solution)/shard_map/erf,efd->erd/dot_general | solution.py:105
  243.0 8.8 %copy.95 = bf16[1,768,1152]{1,0,2:T(2,128)(2,1)} copy(bf16[1,768,1152]{2,1,0:T(8,128)(2,1)} %fusion.15) | data formatting | bytes 3538944
  251.9 3.5 copy.103
  256.2 31.8 %reduce-scatter.4.cloned.1.call-done = bf16[288,768]{1,0:T(8,128)(2,1)} async-done(((bf16[1152,768]{1,0:T(8,128)(2,1)}), bf16[288,768]{1,0:T(8,128)(2,1)}) %reduce-scatter.4.cloned.1.call-update) | async-done | bytes 442384
  290.4 4.6 %copy.90 = bf16[1,768,288]{2,0,1:T(2,128)(2,1)} copy(bf16[1,768,288]{1,2,0:T(8,128)(2,1)} %add_convert_fusion.1) | data formatting | bytes 884736 | tf_op jit(solution)/shard_map/convert_element_type | solution.py:115
  295.5 6.1 %reduce.13 = bf16[768,288]{1,0:T(8,128)(2,1)} reduce(bf16[768,1,288]{2,1,0:T(2,128)(2,1)} %bitcast.121, bf16[]{:T(256)} %broadcast.265), dimensions={1}, to_apply=%bitcast.92.reduce_sub_computation | reduce | bytes 884738
  301.6 2.6 reshape.249
  304.3 18.3 %all_to_all.88 = bf16[8,2,13824]{2,1,0:T(2,128)(2,1)} all-to-all(bf16[8,2,13824]{2,1,0:T(2,128)(2,1)} %reshape.249), channel_id=1, replica_groups=mesh['frame'=8,'tok'=4] {'frame'}, dimensions={0} | all-to-all | bytes 884736 | tf_op jit(solution)/shard_map/all_to_all | solution.py:116
  322.5 3.8 reshape.250
  326.3 4.5 %copy.91 = bf16[1,768,288]{1,2,0:T(8,128)(2,1)} copy(bf16[1,768,288]{2,0,1:T(2,128)(2,1)} %bitcast.122) | data formatting | bytes 884736 | tf_op jit(solution)/shard_map/all_to_all | solution.py:116
  330.8 2.5 all_to_all.80
  334.0 6.5 %gather_fusion.1 = bf16[768]{0:T(1024)(128)(2,1)S(1)} fusion(bf16[8,256]{1,0:T(8,128)(2,1)S(1)} %fusion.28, s32[768]{0:T(1024)S(1)} %reshape.231), kind=kCustom, calls=%fused_computation.1 | custom fusion | bytes 9216 | tf_op jit(solution)/shard_map/jit(take_along_axis)/gather | solution.py:118
  340.5 28.3 %all-gather.2.cloned.1.call-done = bf16[8,96,1152]{1,0,2:T(8,128)(2,1)} async-done(((bf16[8,96,288]{1,0,2:T(8,128)(2,1)}), bf16[8,96,1152]{1,0,2:T(8,128)(2,1)}) %all-gather.2.cloned.1.call-update) | async-done | bytes 1769488 | tf_op jit(solution)/shard_map/all_gather | solution.py:117
  368.8 4.2 %copy.92 = bf16[8,96,1152]{2,1,0:T(8,128)(2,1)} copy(bf16[8,96,1152]{1,0,2:T(8,128)(2,1)} %all-gather.2.cloned.1.call-done) | data formatting | bytes 3538944 | tf_op jit(solution)/shard_map/all_gather | solution.py:117
  373.0 3.3 fusion.24
  (119 shorter events, 57.8 us)
Async XLA Ops:
  6.5 227.7 %copy-start = (bf16[1,1152,1152]{2,1,0:T(8,128)(2,1)S(1)}, bf16[1,1152,1152]{2,1,0:T(8,128)(2,1)}, u32[]{:S(2)}) copy-start(bf16[1,1152,1152]{2,1,0:T(8,128)(2,1)} %param.28) | copy-start | bytes 7962628
  8.8 13.9 %all-to-all-start = ((bf16[4,4,72,256]{3,2,1,0:T(8,128)(2,1)}), bf16[4,4,72,256]{3,2,1,0:T(8,128)(2,1)S(1)}, u32[]{:S(2)}, u32[]{:S(2)}) async-start(bf16[4,4,72,256]{3,2,1,0:T(8,128)(2,1)} %bitcast.128), calls=%async_computation | async-start | bytes 1179648 | tf_op jit(solution)/shard_map/all_to_all | solution.py:75
  14.0 15.2 %copy-start.5 = (s32[8,1,96]{2,1,0:T(1,128)S(1)}, s32[8,1,96]{2,1,0:T(1,128)}, u32[]{:S(2)}) copy-start(s32[8,1,96]{2,1,0:T(1,128)} %param.31) | copy-start | bytes 9220
  22.7 16.7 %copy-start.3 = (f32[1,4,1152]{2,1,0:T(4,128)S(1)}, f32[1,4,1152]{2,1,0:T(4,128)}, u32[]{:S(2)}) copy-start(f32[1,4,1152]{2,1,0:T(4,128)} %param.22) | copy-start | bytes 55300
  22.7 12.4 %all-to-all-start.1 = ((bf16[4,4,72,256]{3,2,1,0:T(8,128)(2,1)}), bf16[4,4,72,256]{3,2,1,0:T(8,128)(2,1)}, u32[]{:S(2)}, u32[]{:S(2)}) async-start(bf16[4,4,72,256]{3,2,1,0:T(8,128)(2,1)} %bitcast.127), calls=%async_computation.1 | async-start | bytes 1179648 | tf_op jit(solution)/shard_map/all_to_all | solution.py:76
  35.1 11.7 %all-to-all-start.2 = ((bf16[4,4,72,256]{3,2,1,0:T(8,128)(2,1)}), bf16[4,4,72,256]{3,2,1,0:T(8,128)(2,1)}, u32[]{:S(2)}, u32[]{:S(2)}) async-start(bf16[4,4,72,256]{3,2,1,0:T(8,128)(2,1)} %bitcast.126), calls=%async_computation.2 | async-start | bytes 1179648 | tf_op jit(solution)/shard_map/all_to_all | solution.py:77
  95.6 6.8 %copy-start.6 = (s32[8,1]{0,1:T(1,128)S(1)}, s32[8,1]{0,1:T(1,128)}, u32[]{:S(2)}) copy-start(s32[8,1]{0,1:T(1,128)} %param.30) | copy-start | bytes 100
  97.9 17.4 %copy-start.7 = (f32[1152]{0:T(1024)S(1)}, f32[1152]{0:T(1024)}, u32[]{:S(2)}) copy-start(f32[1152]{0:T(1024)} %param.24) | copy-start | bytes 13828
  97.9 15.9 %all-to-all-start.3 = ((bf16[1,4,72,1024]{2,1,0,3:T(4,128)(2,1)}), bf16[1,4,72,1024]{2,1,0,3:T(4,128)(2,1)}, u32[]{:S(2)}, u32[]{:S(2)}) async-start(bf16[1,4,72,1024]{2,1,0,3:T(4,128)(2,1)} %bitcast.123), calls=%async_computation.3 | async-start | bytes 2097152 | tf_op jit(solution)/shard_map/all_to_all | solution.py:80
  102.3 131.9 %all-reduce.2.cloned.1.call-start = ((), (), s32[]{:S(2)}) async-start(), calls=%async_computation.7 | async-start | bytes 3538944 | tf_op jit(solution)/shard_map/psum | solution.py:99
  118.4 1.0 copy-start.1
  172.0 0.7 copy-start.4
  172.1 116.0 %reduce-scatter.4.cloned.1.call-start = ((), (), s32[]{:S(2)}) async-start(), calls=%async_computation.9 | async-start | bytes 2211840
  255.4 113.4 %all-gather.2.cloned.1.call-start = ((), (), s32[]{:S(2)}) async-start(), calls=%async_computation.8 | async-start | bytes 2949120 | tf_op jit(solution)/shard_map/all_gather | solution.py:117
  326.3 7.4 %copy-start.2 = (bf16[1152,8]{0,1:T(8,128)(2,1)S(1)}, bf16[1152,8]{0,1:T(8,128)(2,1)}, u32[]{:S(2)}) copy-start(bf16[1152,8]{0,1:T(8,128)(2,1)} %param.25) | copy-start | bytes 55300
Sparse Core Ops, SparseCore 0:
  172.2 61.9 all-reduce.1
  255.5 32.4 reduce-scatter.3
  333.4 35.2 all-gather.1
where the time goes:
time: 385 us; the launch traced here: 383 us
  waiting for transfers between devices  147 us (38%)
  local copies, waits for them, and re-layouts  84.9 us (22%)
  blocking collectives  65.1 us (17%)
  matrix products  25.9 us (7%)
  starting transfers between devices  18.3 us (5%)
  loops' own time  14.9 us (4%)
  other arithmetic  13.9 us (4%)
  between operations  13.3 us (3%)
    psum x1, waiting for transfers between devices, per_device(): lax.psum(moved.astype(jnp.float32).astype(jnp.bfloat16), 'tok')  61.5 us
    all_to_all x1, blocking collectives, per_device(): lax.all_to_all(chosen, 'frame', split_axis=0, concat_axis=1, tiled=True)  46.8 us
    unnamed x4, waiting for transfers between devices  31.9 us
    unnamed x25, local copies, waits for them, and re-layouts  28.5 us
    all_gather x1, waiting for transfers between devices, per_device(): returned_rows = lax.all_gather(returned_cols, 'tok', axis=2, tiled=True)  28.3 us
    all_to_all x1, blocking collectives, per_device(): lax.all_to_all(expert_out, 'frame', split_axis=1, concat_axis=0, tiled=True)  18.3 us
    another operation x4, loops' own time, head_attention(): blocks = lax.map(one_block, starts)  14.8 us
    all_to_all x1, waiting for transfers between devices, per_device(): lax.all_to_all(attended, 'tok', split_axis=3, concat_axis=0, tiled=True)  11.4 us
  transfers between devices with their start and end apart: 7, of which 7 were waited for; matrix products, arithmetic and copies ran while one was open for 5% of the time, Pallas kernels for 0%

commit v1 on v0

--- a/solution.py
+++ b/solution.py
@@ -96,7 +96,9 @@
     chosen = jnp.take(normed, safe_pos, axis=0)
     chosen = jnp.where(on_shard[:, :, None], chosen, jnp.zeros_like(chosen))
     moved = lax.all_to_all(chosen, "frame", split_axis=0, concat_axis=1, tiled=True)
-    expert_rows = lax.psum(moved.astype(jnp.float32).astype(jnp.bfloat16), "tok")
+    expert_rows = jnp.sum(
+        lax.all_gather(moved.astype(jnp.float32).astype(jnp.bfloat16), "tok"), axis=0
+    )
     hidden = jax.nn.gelu(
         jnp.einsum("erd,edf->erf", expert_rows, expand_weight, preferred_element_type=jnp.float32)
         + expand_bias[:, None, :],

time: 385 us -> 403 us (1.047)
  waiting for transfers between devices: 147 us -> 159 us
  other arithmetic: 13.9 us -> 19.7 us
    all_gather x0 -> x1, waiting for transfers between devices: none -> 74 us  [per_device(): lax.all_gather(moved.astype(jnp.float32).astype(jnp.bfloat16), 'tok')]
    psum x1 -> x0, waiting for transfers between devices: 61.5 us -> none  [per_device(): lax.psum(moved.astype(jnp.float32).astype(jnp.bfloat16), 'tok')]
    reduce_sum x0 -> x1, other arithmetic: none -> 5.83 us  [per_device(): jnp.sum(lax.all_gather(moved.astype(jnp.float32).astype(jnp.bfloat16), 't...]
where the time goes in v1:
time: 403 us; the launch traced here: 401 us
  waiting for transfers between devices  159 us (39%)
  local copies, waits for them, and re-layouts  84.9 us (21%)
  blocking collectives  65.1 us (16%)
  matrix products  25.9 us (6%)
  other arithmetic  19.7 us (5%)
  starting transfers between devices  18.3 us (5%)
  loops' own time  14.9 us (4%)
  between operations  13.3 us (3%)
    all_gather x1, waiting for transfers between devices, per_device(): lax.all_gather(moved.astype(jnp.float32).astype(jnp.bfloat16), 'tok')  74 us
    all_to_all x1, blocking collectives, per_device(): lax.all_to_all(chosen, 'frame', split_axis=0, concat_axis=1, tiled=True)  46.8 us
    unnamed x4, waiting for transfers between devices  31.9 us
    unnamed x25, local copies, waits for them, and re-layouts  28.6 us
    all_gather x1, waiting for transfers between devices, per_device(): returned_rows = lax.all_gather(returned_cols, 'tok', axis=2, tiled=True)  28.3 us
    all_to_all x1, blocking collectives, per_device(): lax.all_to_all(expert_out, 'frame', split_axis=1, concat_axis=0, tiled=True)  18.3 us
    another operation x4, loops' own time, head_attention(): blocks = lax.map(one_block, starts)  14.8 us
    all_to_all x1, waiting for transfers between devices, per_device(): lax.all_to_all(attended, 'tok', split_axis=3, concat_axis=0, tiled=True)  11.4 us
  transfers between devices with their start and end apart: 7, of which 7 were waited for; matrix products, arithmetic and copies ran while one was open for 5% of the time, Pallas kernels for 0%

profile of v1, /device:TPU:0, one launch (start us, length us, event | category | flops | bytes accessed | tf_op | source)
XLA Modules:
  0.0 401.3 jit_solution(9132208707262150785)
XLA Ops:
  8.8 5.2 %all-to-all-start = ((bf16[4,4,72,256]{3,2,1,0:T(8,128)(2,1)}), bf16[4,4,72,256]{3,2,1,0:T(8,128)(2,1)S(1)}, u32[]{:S(2)}, u32[]{:S(2)}) async-start(bf16[4,4,72,256]{3,2,1,0:T(8,128)(2,1)} %bitcast.128), calls=%async_computation | async-start | bytes 1179648 | tf_op jit(solution)/shard_map/all_to_all | solution.py:75
  16.1 6.6 %all-to-all-done = bf16[4,4,72,256]{3,2,1,0:T(8,128)(2,1)S(1)} async-done(((bf16[4,4,72,256]{3,2,1,0:T(8,128)(2,1)}), bf16[4,4,72,256]{3,2,1,0:T(8,128)(2,1)S(1)}, u32[]{:S(2)}, u32[]{:S(2)}) %all-to-all-start) | async-done | bytes 589856 | tf_op jit(solution)/shard_map/all_to_all | solution.py:75
  22.7 4.3 %all-to-all-start.1 = ((bf16[4,4,72,256]{3,2,1,0:T(8,128)(2,1)}), bf16[4,4,72,256]{3,2,1,0:T(8,128)(2,1)}, u32[]{:S(2)}, u32[]{:S(2)}) async-start(bf16[4,4,72,256]{3,2,1,0:T(8,128)(2,1)} %bitcast.127), calls=%async_computation.1 | async-start | bytes 1179648 | tf_op jit(solution)/shard_map/all_to_all | solution.py:76
  29.2 5.9 %all-to-all-done.1 = bf16[4,4,72,256]{3,2,1,0:T(8,128)(2,1)} async-done(((bf16[4,4,72,256]{3,2,1,0:T(8,128)(2,1)}), bf16[4,4,72,256]{3,2,1,0:T(8,128)(2,1)}, u32[]{:S(2)}, u32[]{:S(2)}) %all-to-all-start.1) | async-done | bytes 589856 | tf_op jit(solution)/shard_map/all_to_all | solution.py:76
  35.1 4.2 %all-to-all-start.2 = ((bf16[4,4,72,256]{3,2,1,0:T(8,128)(2,1)}), bf16[4,4,72,256]{3,2,1,0:T(8,128)(2,1)}, u32[]{:S(2)}, u32[]{:S(2)}) async-start(bf16[4,4,72,256]{3,2,1,0:T(8,128)(2,1)} %bitcast.126), calls=%async_computation.2 | async-start | bytes 1179648 | tf_op jit(solution)/shard_map/all_to_all | solution.py:77
  49.6 45.9 %while.21 = (s32[]{:T(128)}, bf16[4,72,1024]{2,1,0:T(8,128)(2,1)}, bf16[4,72,1024]{2,1,0:T(8,128)(2,1)}, bf16[4,72,1024]{2,1,0:T(8,128)(2,1)}, bf16[4,72,1024]{2...) while((s32[]{:T(128)}, bf16[4,72,1024]{2,1,0:T(8,128)(2,1)}, ...), condition=%wide.region_5.6_spmd, body=%wide.region_0.5_spmd.sunk | while | flops 155749376 | bytes 8513900 | solution.py:45
  51.6 8.6 %while.22 = (s32[]{:T(128)}, bf16[2,72,512]{2,1,0:T(8,128)(2,1)S(1)}, s32[2]{0:T(128)S(1)}, bf16[72,1024]{1,0:T(8,128)(2,1)S(1)}, bf16[72,1024]{1,0:T(8,128)(2,1...) while((s32[]{:T(128)}, bf16[2,72,512]{2,1,0:T(8,128)(2,1)S(1)}, ...), condition=%wide.region_4.4_spmd, body=%wide.region_1.3_spmd.sunk | while | flops 155749376 | bytes 6744219 | solution.py:40
  63.1 8.6 %while.22 = (s32[]{:T(128)}, bf16[2,72,512]{2,1,0:T(8,128)(2,1)S(1)}, s32[2]{0:T(128)S(1)}, bf16[72,1024]{1,0:T(8,128)(2,1)S(1)}, bf16[72,1024]{1,0:T(8,128)(2,1...) while((s32[]{:T(128)}, bf16[2,72,512]{2,1,0:T(8,128)(2,1)S(1)}, ...), condition=%wide.region_4.4_spmd, body=%wide.region_1.3_spmd.sunk | while | flops 155749376 | bytes 6744219 | solution.py:40
  74.6 8.6 %while.22 = (s32[]{:T(128)}, bf16[2,72,512]{2,1,0:T(8,128)(2,1)S(1)}, s32[2]{0:T(128)S(1)}, bf16[72,1024]{1,0:T(8,128)(2,1)S(1)}, bf16[72,1024]{1,0:T(8,128)(2,1...) while((s32[]{:T(128)}, bf16[2,72,512]{2,1,0:T(8,128)(2,1)S(1)}, ...), condition=%wide.region_4.4_spmd, body=%wide.region_1.3_spmd.sunk | while | flops 155749376 | bytes 6744219 | solution.py:40
  86.0 8.6 %while.22 = (s32[]{:T(128)}, bf16[2,72,512]{2,1,0:T(8,128)(2,1)S(1)}, s32[2]{0:T(128)S(1)}, bf16[72,1024]{1,0:T(8,128)(2,1)S(1)}, bf16[72,1024]{1,0:T(8,128)(2,1...) while((s32[]{:T(128)}, bf16[2,72,512]{2,1,0:T(8,128)(2,1)S(1)}, ...), condition=%wide.region_4.4_spmd, body=%wide.region_1.3_spmd.sunk | while | flops 155749376 | bytes 6744219 | solution.py:40
  97.9 4.4 %all-to-all-start.3 = ((bf16[1,4,72,1024]{2,1,0,3:T(4,128)(2,1)}), bf16[1,4,72,1024]{2,1,0,3:T(4,128)(2,1)}, u32[]{:S(2)}, u32[]{:S(2)}) async-start(bf16[1,4,72,1024]{2,1,0,3:T(4,128)(2,1)} %bitcast.123), calls=%async_computation.3 | async-start | bytes 2097152 | tf_op jit(solution)/shard_map/all_to_all | solution.py:80
  102.5 11.4 %all-to-all-done.3 = bf16[1,4,72,1024]{2,1,0,3:T(4,128)(2,1)} async-done(((bf16[1,4,72,1024]{2,1,0,3:T(4,128)(2,1)}), bf16[1,4,72,1024]{2,1,0,3:T(4,128)(2,1)}, u32[]{:S(2)}, u32[]{:S(2)}) %all-to-all-start.3) | async-done | bytes 589856 | tf_op jit(solution)/shard_map/all_to_all | solution.py:80
  115.4 3.0 fusion.44
  119.8 3.7 gather_fusion
  125.3 46.8 %all_to_all.84 = bf16[8,96,1152]{2,1,0:T(8,128)(2,1)} all-to-all(bf16[8,96,1152]{2,1,0:T(8,128)(2,1)S(1)} %select_select_fusion), channel_id=1, replica_groups=mesh['frame'=8,'tok'=4] {'frame'}, dimensions={0} | all-to-all | bytes 3538944 | tf_op jit(solution)/shard_map/all_to_all | solution.py:98
  172.8 74.0 %all-gather.3.cloned.1.call-done = bf16[4,1,768,1152]{3,2,1,0:T(8,128)(2,1)} async-done(((bf16[1,1,768,1152]{3,2,1,0:T(8,128)(2,1)}), bf16[4,1,768,1152]{3,2,1,0:T(8,128)(2,1)}) %all-gather.3.cloned.1.call-update) | async-done | bytes 7077904 | tf_op jit(solution)/shard_map/all_gather | solution.py:100
  246.8 5.8 %reduce_sum.41 = bf16[768,1152]{1,0:T(8,128)(2,1)} reduce(bf16[4,1,768,1152]{3,2,1,0:T(8,128)(2,1)} %all-gather.3.cloned.1.call-done, bf16[]{:T(256)} %constant.42.clone.1), dimensions={0,1}, to_apply=%region_8.9 | reduce | flops 2654208 | bytes 8847362 | tf_op jit(solution)/shard_map/reduce_sum | solution.py:99
  252.7 8.8 %fusion.15 = bf16[1,768,1152]{2,1,0:T(8,128)(2,1)} fusion(bf16[1,1152,1152]{2,1,0:T(8,128)(2,1)S(1)} %copy-done, bf16[768,1152]{1,0:T(8,128)(2,1)} %reduce_sum.41, bf16[1,1152,1152]{2,1,0:T(8,128)(2,1)} %param.26, f32[1152]{0:T(1024)S(1)} %reduce.7), kind=kOutput, calls=%fused_computation.29 | convolution fusion | flops 4086595584 | bytes 8851968 | tf_op jit(solution)/shard_map/erf,efd->erd/dot_general | solution.py:107
  261.5 8.8 %copy.95 = bf16[1,768,1152]{1,0,2:T(2,128)(2,1)} copy(bf16[1,768,1152]{2,1,0:T(8,128)(2,1)} %fusion.15) | data formatting | bytes 3538944
  270.3 3.5 copy.103
  274.7 31.8 %reduce-scatter.4.cloned.1.call-done = bf16[288,768]{1,0:T(8,128)(2,1)} async-done(((bf16[1152,768]{1,0:T(8,128)(2,1)}), bf16[288,768]{1,0:T(8,128)(2,1)}) %reduce-scatter.4.cloned.1.call-update) | async-done | bytes 442384
  308.8 4.6 %copy.90 = bf16[1,768,288]{2,0,1:T(2,128)(2,1)} copy(bf16[1,768,288]{1,2,0:T(8,128)(2,1)} %add_convert_fusion.1) | data formatting | bytes 884736 | tf_op jit(solution)/shard_map/convert_element_type | solution.py:117
  314.0 6.1 %reduce.15 = bf16[768,288]{1,0:T(8,128)(2,1)} reduce(bf16[768,1,288]{2,1,0:T(2,128)(2,1)} %bitcast.121, bf16[]{:T(256)} %broadcast.265), dimensions={1}, to_apply=%bitcast.92.reduce_sub_computation | reduce | bytes 884738
  320.1 2.6 reshape.248
  322.7 18.3 %all_to_all.85 = bf16[8,2,13824]{2,1,0:T(2,128)(2,1)} all-to-all(bf16[8,2,13824]{2,1,0:T(2,128)(2,1)} %reshape.248), channel_id=1, replica_groups=mesh['frame'=8,'tok'=4] {'frame'}, dimensions={0} | all-to-all | bytes 884736 | tf_op jit(solution)/shard_map/all_to_all | solution.py:118
  341.0 3.8 reshape.249
  344.7 4.5 %copy.91 = bf16[1,768,288]{1,2,0:T(8,128)(2,1)} copy(bf16[1,768,288]{2,0,1:T(2,128)(2,1)} %bitcast.122) | data formatting | bytes 884736 | tf_op jit(solution)/shard_map/all_to_all | solution.py:118
  349.3 2.5 all_to_all.77
  352.4 6.5 %gather_fusion.1 = bf16[768]{0:T(1024)(128)(2,1)S(1)} fusion(bf16[8,256]{1,0:T(8,128)(2,1)S(1)} %fusion.28, s32[768]{0:T(1024)S(1)} %reshape.230), kind=kCustom, calls=%fused_computation.1 | custom fusion | bytes 9216 | tf_op jit(solution)/shard_map/jit(take_along_axis)/gather | solution.py:120
  358.9 28.3 %all-gather.5.cloned.1.call-done = bf16[8,96,1152]{1,0,2:T(8,128)(2,1)} async-done(((bf16[8,96,288]{1,0,2:T(8,128)(2,1)}), bf16[8,96,1152]{1,0,2:T(8,128)(2,1)}) %all-gather.5.cloned.1.call-update) | async-done | bytes 1769488 | tf_op jit(solution)/shard_map/all_gather | solution.py:119
  387.2 4.2 %copy.92 = bf16[8,96,1152]{2,1,0:T(8,128)(2,1)} copy(bf16[8,96,1152]{1,0,2:T(8,128)(2,1)} %all-gather.5.cloned.1.call-done) | data formatting | bytes 3538944 | tf_op jit(solution)/shard_map/all_gather | solution.py:119
  391.4 3.3 fusion.24
  (120 shorter events, 60.2 us)
Async XLA Ops:
  6.5 246.1 %copy-start = (bf16[1,1152,1152]{2,1,0:T(8,128)(2,1)S(1)}, bf16[1,1152,1152]{2,1,0:T(8,128)(2,1)}, u32[]{:S(2)}) copy-start(bf16[1,1152,1152]{2,1,0:T(8,128)(2,1)} %param.28) | copy-start | bytes 7962628
  8.8 13.9 %all-to-all-start = ((bf16[4,4,72,256]{3,2,1,0:T(8,128)(2,1)}), bf16[4,4,72,256]{3,2,1,0:T(8,128)(2,1)S(1)}, u32[]{:S(2)}, u32[]{:S(2)}) async-start(bf16[4,4,72,256]{3,2,1,0:T(8,128)(2,1)} %bitcast.128), calls=%async_computation | async-start | bytes 1179648 | tf_op jit(solution)/shard_map/all_to_all | solution.py:75
  14.0 15.2 %copy-start.5 = (s32[8,1,96]{2,1,0:T(1,128)S(1)}, s32[8,1,96]{2,1,0:T(1,128)}, u32[]{:S(2)}) copy-start(s32[8,1,96]{2,1,0:T(1,128)} %param.31) | copy-start | bytes 9220
  22.7 16.7 %copy-start.3 = (f32[1,4,1152]{2,1,0:T(4,128)S(1)}, f32[1,4,1152]{2,1,0:T(4,128)}, u32[]{:S(2)}) copy-start(f32[1,4,1152]{2,1,0:T(4,128)} %param.22) | copy-start | bytes 55300
  22.7 12.4 %all-to-all-start.1 = ((bf16[4,4,72,256]{3,2,1,0:T(8,128)(2,1)}), bf16[4,4,72,256]{3,2,1,0:T(8,128)(2,1)}, u32[]{:S(2)}, u32[]{:S(2)}) async-start(bf16[4,4,72,256]{3,2,1,0:T(8,128)(2,1)} %bitcast.127), calls=%async_computation.1 | async-start | bytes 1179648 | tf_op jit(solution)/shard_map/all_to_all | solution.py:76
  35.1 11.7 %all-to-all-start.2 = ((bf16[4,4,72,256]{3,2,1,0:T(8,128)(2,1)}), bf16[4,4,72,256]{3,2,1,0:T(8,128)(2,1)}, u32[]{:S(2)}, u32[]{:S(2)}) async-start(bf16[4,4,72,256]{3,2,1,0:T(8,128)(2,1)} %bitcast.126), calls=%async_computation.2 | async-start | bytes 1179648 | tf_op jit(solution)/shard_map/all_to_all | solution.py:77
  95.6 6.8 %copy-start.6 = (s32[8,1]{0,1:T(1,128)S(1)}, s32[8,1]{0,1:T(1,128)}, u32[]{:S(2)}) copy-start(s32[8,1]{0,1:T(1,128)} %param.30) | copy-start | bytes 100
  97.9 17.4 %copy-start.7 = (f32[1152]{0:T(1024)S(1)}, f32[1152]{0:T(1024)}, u32[]{:S(2)}) copy-start(f32[1152]{0:T(1024)} %param.24) | copy-start | bytes 13828
  97.9 15.9 %all-to-all-start.3 = ((bf16[1,4,72,1024]{2,1,0,3:T(4,128)(2,1)}), bf16[1,4,72,1024]{2,1,0,3:T(4,128)(2,1)}, u32[]{:S(2)}, u32[]{:S(2)}) async-start(bf16[1,4,72,1024]{2,1,0,3:T(4,128)(2,1)} %bitcast.123), calls=%async_computation.3 | async-start | bytes 2097152 | tf_op jit(solution)/shard_map/all_to_all | solution.py:80
  102.3 144.5 %all-gather.3.cloned.1.call-start = ((), (), s32[]{:S(2)}) async-start(), calls=%async_computation.7 | async-start | bytes 8847360 | tf_op jit(solution)/shard_map/all_gather | solution.py:100
  118.4 1.1 copy-start.1
  172.1 0.7 copy-start.4
  172.1 134.3 %reduce-scatter.4.cloned.1.call-start = ((), (), s32[]{:S(2)}) async-start(), calls=%async_computation.9 | async-start | bytes 2211840
  273.8 113.4 %all-gather.5.cloned.1.call-start = ((), (), s32[]{:S(2)}) async-start(), calls=%async_computation.8 | async-start | bytes 2949120 | tf_op jit(solution)/shard_map/all_gather | solution.py:119
  344.7 7.4 %copy-start.2 = (bf16[1152,8]{0,1:T(8,128)(2,1)S(1)}, bf16[1152,8]{0,1:T(8,128)(2,1)}, u32[]{:S(2)}) copy-start(bf16[1152,8]{0,1:T(8,128)(2,1)} %param.25) | copy-start | bytes 55300
Sparse Core Ops, SparseCore 0:
  172.3 74.5 all-gather.2
  274.0 32.4 reduce-scatter.3
  351.9 35.2 all-gather.4
